TPU v7x, 256 devices: a whole 4x4x8 slice. The times are simulated.
256 devices in a mesh: dp: 64 (over x, z, core), proto: 4 (over y).
Axes of the slice: x: 4, y: 4, z: 8, core: 2. Of those that a mesh axis runs over, the one named last changes fastest.
Arguments:
- embeddings: bfloat16 [65536, 1024], P(('dp', 'proto')), may hold values from -6 to 6
- centres: bfloat16 [8192, 1024], P('proto'), may hold values from -0.1875 to 0.1875
Outputs:
- updated: bfloat16 [8192, 1024], P('proto')
All inputs are finite; a program needn't handle non-finite values.
Results may differ from a plain program's by a relative error of at most 0.0074.
Values may be sent and summed in bfloat16 or wider, within the bound.
A program may use at most 64 MiB of HBM per device.

v0:
```python
import jax
import jax.numpy as jnp
from jax import lax
from jax.sharding import PartitionSpec as P

ITERS = 3


def normalise(rows):
    values = rows.astype(jnp.float32)
    scaled = values * lax.rsqrt(jnp.mean(values * values, axis=1, keepdims=True) + 1e-05)
    return scaled.astype(jnp.bfloat16)


def column_total(partial_sum):
    return lax.psum(partial_sum, "dp")


def row_total(partial_sum):
    return lax.psum(partial_sum, "proto")


def per_device(embeddings, centres):
    unit = normalise(embeddings)
    group = lax.all_gather(unit, "proto", axis=0, tiled=True)
    scores = lax.dot_general(
        group, centres, (((1,), (1,)), ((), ())), preferred_element_type=jnp.float32
    )
    plan = jnp.exp(4.0 * scores)
    total_rows = group.shape[0] * lax.axis_size("dp")
    total_cols = centres.shape[0] * lax.axis_size("proto")
    for step in range(ITERS):
        colsum = column_total(jnp.sum(plan, axis=0))
        plan = plan / (total_cols * colsum)[None, :]
        rowsum = row_total(jnp.sum(plan, axis=1))
        plan = plan / (total_rows * rowsum)[:, None]
    codes = (total_rows * plan).astype(jnp.bfloat16)
    share = lax.psum_scatter(
        lax.dot_general(codes, group, (((0,), (0,)), ((), ())), preferred_element_type=jnp.float32),
        "dp",
        scatter_dimension=0,
        tiled=True,
    )
    rescaled = share * lax.rsqrt(jnp.mean(share * share, axis=1, keepdims=True) + 1e-05)
    return lax.all_gather(rescaled.astype(jnp.bfloat16), "dp", axis=0, tiled=True)


def solution(mesh):
    return jax.shard_map(
        per_device,
        mesh=mesh,
        in_specs=(P(("dp", "proto"), None), P("proto", None)),
        out_specs=P("proto", None),
        check_vma=False,
    )
```

profile of v0, /device:TPU:1, one launch (start us, length us, event | category | flops | bytes accessed | tf_op | source)
XLA Modules:
  0.0 737.2 jit_solution(6118723697224441080)
XLA Ops:
  6.5 0.0 all-gather.3.cloned.1.call-start
  6.5 1.2 fusion.15
  7.8 2.0 fusion.16
  9.8 0.0 all-gather.3.cloned.1.call-update
  9.8 0.0 reduce-scatter.2.cloned.1.call-start
  9.8 37.1 %all-gather.3.cloned.1.call-done = bf16[1024,1024]{1,0:T(8,128)(2,1)} async-done(((bf16[256,1024]{1,0:T(8,128)(2,1)}), bf16[1024,1024]{1,0:T(8,128)(2,1)}) %all-gather.3.cloned.1.call-update) | async-done | bytes 2097168 | tf_op jit(solution)/shard_map/all_gather | solution.py:25
  46.9 10.6 %fusion.18 = (f32[2048]{0:T(1024)S(1)}, f32[1024,2048]{1,0:T(8,128)}) fusion(bf16[1024,1024]{1,0:T(8,128)(2,1)} %all-gather.3.cloned.1.call-done, bf16[2048,1024]{1,0:T(8,128)(2,1)} %param.3), kind=kOutput, calls=%fused_computation.33 | convolution fusion | flops 4299159552 | bytes 14688256 | tf_op jit(solution)/shard_map/dot_general | solution.py:26
  57.5 126.7 %psum.42 = f32[2048]{0:T(1024)S(1)} all-reduce(f32[2048]{0:T(1024)S(1)} %get-tuple-element.5), channel_id=1, replica_groups=mesh['dp'=64,'proto'=4] {'dp'}, use_global_device_ids=true, to_apply=%region_2.0 | all-reduce | flops 2048 | bytes 16384 | tf_op jit(solution)/shard_map/psum | solution.py:16
  184.3 4.0 divide_reduce_fusion
  188.3 6.6 psum.43
  194.9 4.2 fusion.8
  199.0 132.3 %psum.44 = f32[2048]{0:T(1024)S(1)} all-reduce(f32[2048]{0:T(1024)S(1)} %fusion.8), channel_id=1, replica_groups=mesh['dp'=64,'proto'=4] {'dp'}, use_global_device_ids=true, to_apply=%region_6.0 | all-reduce | flops 2048 | bytes 16384 | tf_op jit(solution)/shard_map/psum | solution.py:16
  331.4 4.4 fusion.10
  335.8 6.9 psum.45
  342.7 0.0 copy-start
  342.7 4.6 fusion.11
  347.3 128.1 %psum.46 = f32[2048]{0:T(1024)S(1)} all-reduce(f32[2048]{0:T(1024)S(1)} %fusion.11), channel_id=1, replica_groups=mesh['dp'=64,'proto'=4] {'dp'}, use_global_device_ids=true, to_apply=%region_10.0 | all-reduce | flops 2048 | bytes 16384 | tf_op jit(solution)/shard_map/psum | solution.py:16
  475.4 4.7 fusion.12
  480.1 6.6 psum.47
  486.7 0.0 copy-done
  486.7 12.4 %fusion.13 = f32[2048,1024]{1,0:T(8,128)} fusion(bf16[1024,1024]{1,0:T(8,128)(2,1)S(1)} %copy-done, f32[1024,2048]{1,0:T(8,128)} %get-tuple-element.6, f32[1024]{0:T(1024)S(1)} %broadcast_multiply_fusion.3, f32[2048]{0:T(1024)S(1)} %broadcast_multiply_fusion, f32[1024]{0:T(1024)S(1)} %broadcast_multiply_fusion.4, f32[2048]{0:T(1024)S(1)} %broadcast_multiply_fusion.1, ...), kind=kOutput, calls=%fused_computation.17 | convolution fusion | flops 4311744512 | bytes 18911232 | tf_op jit(solution)/shard_map/dot_general | solution.py:39
  499.1 0.0 reduce-scatter.2.cloned.1.call-update
  499.2 0.0 all-gather.5.cloned.1.call-start
  499.2 141.6 %reduce-scatter.2.cloned.1.call-done = f32[32,1024]{1,0:T(8,128)} async-done(((f32[2048,1024]{1,0:T(8,128)}), f32[32,1024]{1,0:T(8,128)}) %reduce-scatter.2.cloned.1.call-update) | async-done | bytes 131088 | tf_op jit(solution)/shard_map/reduce_scatter | solution.py:38
  640.8 1.0 multiply_reduce_fusion
  641.8 1.6 multiply_convert_fusion
  643.4 0.0 all-gather.5.cloned.1.call-update
  643.5 82.6 %all-gather.5.cloned.1.call-done = bf16[2048,1024]{1,0:T(8,128)(2,1)} async-done(((bf16[32,1024]{1,0:T(8,128)(2,1)}), bf16[2048,1024]{1,0:T(8,128)(2,1)}) %all-gather.5.cloned.1.call-update) | async-done | bytes 4194320 | tf_op jit(solution)/shard_map/all_gather | solution.py:45
  726.1 4.6 copy.4
  (8 shorter events, 0.0 us)
Async XLA Ops:
  6.5 40.4 %all-gather.3.cloned.1.call-start = ((), (), s32[]{:S(2)}) async-start(), calls=%async_computation.1 | async-start | bytes 2621440 | tf_op jit(solution)/shard_map/all_gather | solution.py:25
  9.8 631.0 %reduce-scatter.2.cloned.1.call-start = ((), (), s32[]{:S(2)}) async-start(), calls=%async_computation.2 | async-start | bytes 8519680 | tf_op jit(solution)/shard_map/reduce_scatter | solution.py:38
  342.7 144.0 %copy-start = (bf16[1024,1024]{1,0:T(8,128)(2,1)S(1)}, bf16[1024,1024]{1,0:T(8,128)(2,1)}, u32[]{:S(2)}) copy-start(bf16[1024,1024]{1,0:T(8,128)(2,1)} %all-gather.3.cloned.1.call-done) | copy-start | bytes 6291460
  499.2 226.9 %all-gather.5.cloned.1.call-start = ((), (), s32[]{:S(2)}) async-start(), calls=%async_computation.3 | async-start | bytes 4259840 | tf_op jit(solution)/shard_map/all_gather | solution.py:45
Sparse Core Ops, SparseCore 0:
  9.9 36.9 all-gather.2
  499.3 141.4 reduce-scatter.1
  643.6 82.4 all-gather.4
where the time goes:
time: 738 us; the launch traced here: 737 us
  blocking collectives  407 us (55%)
  waiting for transfers between devices  261 us (35%)
  other arithmetic  27.7 us (4%)
  matrix products  23.1 us (3%)
  between operations  13.2 us (2%)
    psum x3, blocking collectives, column_total(): return lax.psum(partial_sum, 'dp')  387 us
    reduce_scatter x1, waiting for transfers between devices, per_device(): lax.psum_scatter(lax.dot_general(codes, group, (((0,), (0,)), ((), ())),...  142 us
    all_gather x1, waiting for transfers between devices, per_device(): lax.all_gather(rescaled.astype(jnp.bfloat16), 'dp', axis=0, tiled=True)  82.6 us
    all_gather x1, waiting for transfers between devices, per_device(): group = lax.all_gather(unit, 'proto', axis=0, tiled=True)  37.1 us
    psum x3, blocking collectives, row_total(): return lax.psum(partial_sum, 'proto')  20 us
  transfers between devices with their start and end apart: 3, of which 3 were waited for; matrix products, arithmetic and copies ran while one was open for 0% of the time, Pallas kernels for 0%

commit v1 on v0

v1 whole, which is shorter than its diff:
```python
import jax
import jax.numpy as jnp
from jax import lax
from jax.experimental import pallas as pl
from jax.experimental.pallas import tpu as pltpu
from jax.sharding import PartitionSpec as P

ITERS = 3
NX, NZ, NC, NY = 4, 8, 2, 4
F32, BF16 = jnp.float32, jnp.bfloat16
VMEM, DMA = pltpu.VMEM, pltpu.SemaphoreType.DMA


def remote(src, dst, send, recv, device):
    return pltpu.make_async_remote_copy(
        src_ref=src, dst_ref=dst, send_sem=send, recv_sem=recv,
        device_id=device, device_id_type=pl.DeviceIdType.MESH,
    )


def rescale(values):
    return values * lax.rsqrt(jnp.mean(values * values, axis=1, keepdims=True) + 1e-05)


class ScatterRing:
    def __init__(self, n, me, device, load, size, send, recv, ssem, rsem):
        self.n, self.me, self.device, self.load, self.size = n, me, device, load, size
        self.send_buf, self.recv_buf, self.ssem, self.rsem = send, recv, ssem, rsem
        self.half = send.shape[-1] // 2
        self.copies = {}

    def step(self, k):
        n, half, far = self.n, self.half, self.n // 2
        for d, sign in ((0, 1), (1, n - 1)):
            if k < far:
                self.copies[d, k + 1].wait_recv()
            block = lax.rem(self.me + (sign * k) % n, n)
            cols = pl.ds(d * half, half) if k == far else pl.ds(0, 2 * half)

            @pl.loop(0, self.size // 16)
            def _(i, d=d, block=block):
                rows = pl.ds(pl.multiple_of(i * 16, 16), 16)
                if k == far:
                    total = self.load(block, i, cols)
                    self.send_buf[d, k - 1, rows, cols] = total.astype(BF16)
                elif k == far - 1:
                    for h in range(2):
                        part = pl.ds(h * half, half)
                        total = self.load(block, i, part)
                        if h == d:
                            total = total + self.recv_buf[d, k, rows, part].astype(F32)
                        self.send_buf[d, k - 1, rows, part] = total.astype(BF16)
                else:
                    total = self.load(block, i, cols) + self.recv_buf[d, k, rows, :].astype(F32)
                    self.send_buf[d, k - 1, rows, :] = total.astype(BF16)

            copy = remote(
                self.send_buf.at[d, k - 1, :, cols], self.recv_buf.at[d, k - 1, :, cols],
                self.ssem.at[d, k - 1], self.rsem.at[d, k - 1],
                self.device(lax.rem(self.me + sign, n)),
            )
            copy.start()
            self.copies[d, k] = copy

    def finish(self, store):
        for d in range(2):
            self.copies[d, 1].wait_recv()

        @pl.loop(0, self.size // 16)
        def _(i):
            rows = pl.ds(pl.multiple_of(i * 16, 16), 16)
            total = self.load(self.me, i, pl.ds(0, 2 * self.half))
            for d in range(2):
                if self.n == 2 * 1:
                    continue
                total = total + self.recv_buf[d, 0, rows, :].astype(F32)
            store(i, total)

    def drain(self):
        for copy in self.copies.values():
            copy.wait_send()


class GatherRing:
    def __init__(self, n, me, device, base, size, out, ssem, rsem):
        self.n, self.me, self.device, self.base, self.size = n, me, device, base, size
        self.out, self.ssem, self.rsem = out, ssem, rsem
        self.half = out.shape[-1] // 2
        self.copies = {}

    def view(self, block, cols):
        start = pl.multiple_of(self.base + block * self.size, 16)
        return self.out.at[pl.ds(start, self.size), cols]

    def cols(self, d, k):
        return pl.ds(d * self.half, self.half) if k == self.n // 2 else pl.ds(0, 2 * self.half)

    def source(self, d, k):
        back = (self.n - k) % self.n if d == 0 else k % self.n
        return lax.rem(self.me + back, self.n)

    def step(self, k):
        for d, sign in ((0, 1), (1, self.n - 1)):
            view = self.view(self.source(d, k - 1), self.cols(d, k))
            copy = remote(
                view, view, self.ssem.at[d, k - 1], self.rsem.at[d, k - 1],
                self.device(lax.rem(self.me + sign, self.n)),
            )
            copy.start()
            self.copies[d, k] = copy

    def arrive(self, k):
        for d in range(2):
            self.copies[d, k].wait_recv()

    def drain(self):
        for copy in self.copies.values():
            copy.wait_send()


def kernel(
    emb_hbm, cen_hbm, out_hbm,
    emb, cen, unit, plan, scale_b, col_acc, row_scale,
    col_v, col_c, col_x, col_z, row_v, row_r,
    mate_s, mate_r, own, own_a, own_b,
    ax_s, ax_r, az_s, az_r, bz_s, bz_r, bx_s, bx_r, out,
    local_sem, unit_ss, unit_rs, col_ss, col_rs, row_ss, row_rs, mate_ss, mate_rs,
    ax_ss, ax_rs, az_ss, az_rs, bz_ss, bz_rs, bx_ss, bx_rs,
    gaz_ss, gaz_rs, gax_ss, gax_rs, gbx_ss, gbx_rs, gbz_ss, gbz_rs, fwd_ss, fwd_rs,
):
    rows, width = emb.shape
    protos = cen.shape[0]
    dp, y = lax.axis_index("dp"), lax.axis_index("proto")
    core = lax.rem(dp, NC)
    chip = lax.div(dp, NC)
    z, x = lax.rem(chip, NZ), lax.div(chip, NZ)
    mate = 1 - core

    def at(x, z, core):
        return ((x * NZ + z) * NC + core, y)

    def x_device(k):
        return at(k, z, core)

    def z_device(k):
        return at(x, k, core)

    mate_device = at(x, z, mate)
    x_peers = [x_device(lax.rem(x + k, NX)) for k in range(1, NX)]
    z_peers = [z_device(lax.rem(z + k, NZ)) for k in range(1, NZ)]
    y_peers = [(dp, lax.rem(y + k, NY)) for k in range(1, NY)]
    peers = [mate_device] + x_peers + z_peers + y_peers

    load_emb = pltpu.make_async_copy(emb_hbm, emb, local_sem.at[0])
    load_cen = pltpu.make_async_copy(cen_hbm, cen, local_sem.at[1])
    load_emb.start()
    load_cen.start()
    barrier = pltpu.get_barrier_semaphore()
    for peer in peers:
        pl.semaphore_signal(barrier, inc=1, device_id=peer, device_id_type=pl.DeviceIdType.MESH)
    load_emb.wait()

    @pl.loop(0, rows // 32)
    def _(i):
        part = pl.ds(pl.multiple_of(i * 32, 32), 32)
        unit[y, part, :] = rescale(emb[part, :].astype(F32)).astype(BF16)

    pl.semaphore_wait(barrier, len(peers))

    right, left, far = (lax.rem(y + k, NY) for k in (1, 3, 2))
    half = rows // 2

    def send_unit(index, block, which, to):
        view = unit.at[block, pl.ds(which * half, half), :]
        copy = remote(view, view, unit_ss.at[index], unit_rs.at[index], (dp, to))
        copy.start()
        return copy

    def scores(block, first):
        step = 256

        @pl.loop(0, protos // step)
        def _(i):
            js = pl.ds(pl.multiple_of(i * step, step), step)
            s = lax.dot_general(
                cen[js, :], unit[block], (((1,), (1,)), ((), ())), preferred_element_type=F32
            )
            p = jnp.exp(4.0 * s)
            plan[block, js, :] = p
            part = p[:, :128] + p[:, 128:]
            col_acc[js, :] = part if first else col_acc[js, :] + part

    ups = [send_unit(0, y, 0, right), send_unit(3, y, 1, left), send_unit(1, y, 1, right), send_unit(4, y, 0, left)]
    load_cen.wait()
    scores(y, True)
    ups[0].wait_recv()
    ups.append(send_unit(2, left, 0, right))
    ups[1].wait_recv()
    ups.append(send_unit(5, right, 1, left))
    ups[2].wait_recv()
    scores(left, False)
    ups[3].wait_recv()
    scores(right, False)
    ups[4].wait_recv()
    ups[5].wait_recv()
    scores(far, False)

    groups = protos // 128

    def lane_total(part):
        return jnp.sum(jnp.transpose(part), axis=0, keepdims=True)

    @pl.loop(0, groups)
    def _(g):
        col_v[0, 0, pl.ds(g, 1), :] = lane_total(col_acc[pl.ds(pl.multiple_of(g * 128, 128), 128), :])

    @pl.loop(0, ITERS)
    def _(t):
        copy = remote(col_v.at[t, 0], col_c.at[t], col_ss.at[t, 0], col_rs.at[t, 0], mate_device)
        copy.start()
        copy.wait()
        col_v[t, 1] = col_v[t, 0] + col_c[t]
        copies = [
            remote(col_v.at[t, 1], col_x.at[t, i], col_ss.at[t, 1 + i], col_rs.at[t, 1 + i], peer)
            for i, peer in enumerate(x_peers)
        ]
        for copy in copies:
            copy.start()
        for copy in copies:
            copy.wait()
        total = col_v[t, 1]
        for i in range(NX - 1):
            total = total + col_x[t, i]
        col_v[t, 2] = total
        copies = [
            remote(col_v.at[t, 2], col_z.at[t, i], col_ss.at[t, NX + i], col_rs.at[t, NX + i], peer)
            for i, peer in enumerate(z_peers)
        ]
        for copy in copies:
            copy.start()
        for copy in copies:
            copy.wait()
        total = col_v[t, 2]
        for i in range(NZ - 1):
            total = total + col_z[t, i]
        col_v[t, 3] = 1.0 / total

        def row_step(g, accs):
            js = pl.ds(pl.multiple_of(g * 128, 128), 128)
            spread = jnp.transpose(jnp.broadcast_to(col_v[t, 3, pl.ds(g, 1), :], (128, 128)))
            scale_b[js, :] = spread
            spread = jnp.concatenate([spread, spread], axis=1)
            return tuple(
                acc + jnp.sum((plan[b, js, :] * spread).reshape(16, 8, rows), axis=0)
                for b, acc in enumerate(accs)
            )

        accs = lax.fori_loop(0, groups, row_step, tuple(jnp.zeros((8, rows), F32) for _ in range(NY)))
        for b in range(NY):
            total = jnp.sum(accs[b], axis=0, keepdims=True)
            row_v[t, 2 * b : 2 * b + 1, :] = total[:, :128]
            row_v[t, 2 * b + 1 : 2 * b + 2, :] = total[:, 128:]
        copies = [
            remote(row_v.at[t], row_r.at[t, i], row_ss.at[t, i], row_rs.at[t, i], peer)
            for i, peer in enumerate(y_peers)
        ]
        for copy in copies:
            copy.start()
        for copy in copies:
            copy.wait()
        total = row_v[t]
        for i in range(NY - 1):
            total = total + row_r[t, i]
        row_scale[...] = 1.0 / total

        @pl.when(t < ITERS - 1)
        def _():
            @pl.loop(0, groups)
            def _(g):
                js = pl.ds(pl.multiple_of(g * 128, 128), 128)
                spread = scale_b[js, :]
                part = jnp.zeros((128, 128), F32)
                for b in range(NY):
                    for h in range(2):
                        lanes = pl.ds(h * 128, 128)
                        p = plan[b, js, lanes] * spread * row_scale[2 * b + h : 2 * b + h + 1, :]
                        plan[b, js, lanes] = p
                        part = part + p
                col_v[t + 1, 0, pl.ds(g, 1), :] = lane_total(part)

    step = 256
    mine = protos // 2
    all_unit = unit.reshape(NY * rows, width)

    def partial_sums(start):
        js = pl.ds(pl.multiple_of(start, step), step)
        spread = scale_b[js, :]
        codes = jnp.concatenate(
            [
                (plan[b, js, h * 128 : h * 128 + 128] * spread * row_scale[2 * b + h : 2 * b + h + 1, :]).astype(BF16)
                for b in range(NY)
                for h in range(2)
            ],
            axis=1,
        )
        return jnp.dot(codes, all_unit[...], preferred_element_type=F32)

    def mate_copy(q):
        view = pl.ds(pl.multiple_of(q * step, step), step)
        return remote(mate_s.at[view, :], mate_r.at[view, :], mate_ss.at[q], mate_rs.at[q], mate_device)

    @pl.loop(0, mine // step)
    def _(q):
        view = pl.ds(pl.multiple_of(q * step, step), step)
        mate_s[view, :] = partial_sums(mate * mine + q * step).astype(BF16)
        mate_copy(q).start()

    @pl.loop(0, mine // step)
    def _(q):
        view = pl.ds(pl.multiple_of(q * step, step), step)
        total = partial_sums(core * mine + q * step)
        mate_copy(q).wait_recv()
        own[view, :] = total + mate_r[view, :].astype(F32)

    part = mine // 2
    ax_size, bz_size = part // NX, part // NZ
    size = part // (NX * NZ)

    def loader(ref, base, size):
        def load(block, i, cols):
            return ref[pl.ds(pl.multiple_of(base + block * size + i * 16, 16), 16), cols]

        return load

    ax = ScatterRing(NX, x, x_device, loader(own, 0, ax_size), ax_size, ax_s, ax_r, ax_ss, ax_rs)
    bz = ScatterRing(NZ, z, z_device, loader(own, part, bz_size), bz_size, bz_s, bz_r, bz_ss, bz_rs)
    az = ScatterRing(NZ, z, z_device, loader(own_a, 0, size), size, az_s, az_r, az_ss, az_rs)
    bx = ScatterRing(NX, x, x_device, loader(own_b, 0, size), size, bx_s, bx_r, bx_ss, bx_rs)

    def keep(ref):
        def store(i, total):
            ref[pl.ds(pl.multiple_of(i * 16, 16), 16), :] = total

        return store

    def deliver(base):
        def store(i, total):
            out[pl.ds(pl.multiple_of(base + i * 16, 16), 16), :] = rescale(total).astype(BF16)

        return store

    base_a = core * mine
    base_b = base_a + part
    bz.step(4)
    ax.step(2)
    bz.step(3)
    ax.step(1)
    bz.step(2)
    bz.step(1)
    ax.finish(keep(own_a))
    az.step(4)
    bz.finish(keep(own_b))
    bx.step(2)
    az.step(3)
    bx.step(1)
    az.step(2)
    az.step(1)
    bx.finish(deliver(base_b + z * bz_size + x * size))
    gbx = GatherRing(NX, x, x_device, base_b + z * bz_size, size, out, gbx_ss, gbx_rs)
    gbx.step(1)
    az.finish(deliver(base_a + x * ax_size + z * size))
    gaz = GatherRing(NZ, z, z_device, base_a + x * ax_size, size, out, gaz_ss, gaz_rs)
    gaz.step(1)

    gax = GatherRing(NX, x, x_device, base_a, ax_size, out, gax_ss, gax_rs)
    gbz = GatherRing(NZ, z, z_device, base_b, bz_size, out, gbz_ss, gbz_rs)
    forwards = []

    def forward(view):
        index = len(forwards)
        copy = remote(view, view, fwd_ss.at[index], fwd_rs.at[index], mate_device)
        copy.start()
        forwards.append(copy)

    def forward_arrived(ring, k):
        ring.arrive(k)
        if k < ring.n // 2:
            ring.step(k + 1)
        for d in range(2):
            forward(ring.view(ring.source(d, k), ring.cols(d, k)))

    gbx.arrive(1)
    gbx.step(2)
    gaz.arrive(1)
    gaz.step(2)
    gbx.arrive(2)
    gbz.step(1)
    forward(gbz.view(z, pl.ds(0, width)))
    gaz.arrive(2)
    gaz.step(3)
    gaz.arrive(3)
    gaz.step(4)
    forward_arrived(gbz, 1)
    gaz.arrive(4)
    gax.step(1)
    forward(gax.view(x, pl.ds(0, width)))
    forward_arrived(gbz, 2)
    forward_arrived(gax, 1)
    forward_arrived(gbz, 3)
    forward_arrived(gax, 2)
    forward_arrived(gbz, 4)
    for copy in forwards:
        copy.wait_recv()
    store = pltpu.make_async_copy(out, out_hbm, local_sem.at[2])
    store.start()
    for copy in ups + forwards:
        copy.wait_send()
    for ring in (ax, bz, az, bx, gbx, gaz, gax, gbz):
        ring.drain()

    @pl.loop(0, mine // step)
    def _(q):
        mate_copy(q).wait_send()

    store.wait()


def per_device(embeddings, centres):
    rows, width = embeddings.shape
    protos = centres.shape[0]
    mine = protos // 2
    part = mine // 2
    ax_size, bz_size = part // NX, part // NZ
    size = part // (NX * NZ)
    rings = [(NX, ax_size), (NZ, size), (NZ, bz_size), (NX, size)]
    scratch = [
        VMEM((rows, width), BF16),
        VMEM((protos, width), BF16),
        VMEM((NY, rows, width), BF16),
        VMEM((NY, protos, rows), F32),
        VMEM((protos, 128), F32),
        VMEM((protos, 128), F32),
        VMEM((8, 128), F32),
        VMEM((ITERS, 4, protos // 128, 128), F32),
        VMEM((ITERS, protos // 128, 128), F32),
        VMEM((ITERS, NX - 1, protos // 128, 128), F32),
        VMEM((ITERS, NZ - 1, protos // 128, 128), F32),
        VMEM((ITERS, 8, 128), F32),
        VMEM((ITERS, NY - 1, 8, 128), F32),
        VMEM((mine, width), BF16),
        VMEM((mine, width), BF16),
        VMEM((mine, width), F32),
        VMEM((ax_size, width), F32),
        VMEM((bz_size, width), F32),
    ]
    for n, block in rings:
        scratch += [VMEM((2, n // 2, block, width), BF16)] * 2
    scratch += [VMEM((protos, width), BF16)]
    pairs = [(6,), (ITERS, 1 + NX - 1 + NZ - 1), (ITERS, NY - 1), (4,)]
    pairs += [(2, n // 2) for n, _ in rings]
    pairs += [(2, NZ // 2), (2, NX // 2), (2, NX // 2), (2, NZ // 2), (14,)]
    scratch += [DMA((3,))]
    for shape in pairs:
        scratch += [DMA(shape)] * 2
    return pl.pallas_call(
        kernel,
        out_shape=jax.ShapeDtypeStruct((protos, width), BF16),
        in_specs=[pl.BlockSpec(memory_space=pl.ANY)] * 2,
        out_specs=pl.BlockSpec(memory_space=pl.ANY),
        scratch_shapes=scratch,
        compiler_params=pltpu.CompilerParams(
            collective_id=0, has_side_effects=True, vmem_limit_bytes=60 * 1024 * 1024
        ),
    )(embeddings, centres)


def solution(mesh):
    return jax.shard_map(
        per_device,
        mesh=mesh,
        in_specs=(P(("dp", "proto"), None), P("proto", None)),
        out_specs=P("proto", None),
        check_vma=False,
    )
```

time: 738 us -> 153 us (0.21)
  blocking collectives: 407 us -> 0 us
  waiting for transfers between devices: 261 us -> 0 us
  Pallas kernels: 0 us -> 149 us
  other arithmetic: 27.7 us -> 0 us
  matrix products: 23.1 us -> 0 us
  between operations: 13.2 us -> 0.01 us
    psum x6 -> x0, blocking collectives: 407 us -> none  [the longest x3 387 us: column_total(): return lax.psum(partial_sum, 'dp')]
    pallas_call x0 -> x1, Pallas kernels: none -> 149 us  [per_device(): pl.pallas_call(kernel, out_shape=jax.ShapeDtypeStruct((protos, width), BF...]
    reduce_scatter x1 -> x0, waiting for transfers between devices: 142 us -> none  [per_device(): lax.psum_scatter(lax.dot_general(codes, group, (((0,), (0,)), ((), ())),...]
    all_gather x2 -> x0, waiting for transfers between devices: 120 us -> none  [the longest x1 82.6 us: per_device(): lax.all_gather(rescaled.astype(jnp.bfloat16), 'dp', axis=0, tiled=True)]
    reduce_sum x7 -> x0, other arithmetic: 24.1 us -> none  [the longest x3 13 us: per_device(): rowsum = row_total(jnp.sum(plan, axis=1))]
    dot_general x2 -> x0, matrix products: 23.1 us -> none  [the longest x1 12.4 us: per_device(): lax.dot_general(codes, group, (((0,), (0,)), ((), ())), preferred_element...]
  transfers between devices with their start and end apart: 3 -> 0, of which waited for: 3 -> 0; matrix products, arithmetic and copies ran while one was open for 0% -> 0% of each run, Pallas kernels for 0% -> 0%
where the time goes in v1:
time: 153 us
  Pallas kernels  149 us (97%)
  local copies, waits for them, and re-layouts  4.64 us (3%)
    pallas_call x1, Pallas kernels, per_device(): pl.pallas_call(kernel, out_shape=jax.ShapeDtypeStruct((protos, width), BF...  149 us
    unnamed x1, local copies, waits for them, and re-layouts  4.64 us

profile of v1, /device:TPU:1, one launch (start us, length us, event | category | flops | bytes accessed | tf_op | source)
XLA Modules:
  0.0 153.4 jit_solution(12964433496629974339)
XLA Ops:
  0.0 148.7 %shard_map.28 = bf16[2048,1024]{1,0:T(8,128)(2,1)} custom-call(bf16[256,1024]{1,0:T(8,128)(2,1)} %emb_hbm.1, bf16[2048,1024]{1,0:T(8,128)(2,1)} %cen_hbm.1), custom_call_target="tpu_custom_call" | custom-call | tf_op jit(solution)/shard_map/pallas_call | solution.py:465
  148.7 4.6 %copy.4 = bf16[2048,1024]{1,0:T(8,128)(2,1)} copy(bf16[2048,1024]{1,0:T(8,128)(2,1)} %shard_map.28) | data formatting | bytes 8388608

commit v2 on v1

--- a/solution.py
+++ b/solution.py
@@ -7,6 +7,7 @@
 
 ITERS = 3
 NX, NZ, NC, NY = 4, 8, 2, 4
+WINDOWS = 2
 F32, BF16 = jnp.float32, jnp.bfloat16
 VMEM, DMA = pltpu.VMEM, pltpu.SemaphoreType.DMA
 
@@ -23,58 +24,60 @@
 
 
 class ScatterRing:
-    def __init__(self, n, me, device, load, size, send, recv, ssem, rsem):
+    def __init__(self, n, me, device, load, size, send, recv, ssem, rsem, window):
         self.n, self.me, self.device, self.load, self.size = n, me, device, load, size
         self.send_buf, self.recv_buf, self.ssem, self.rsem = send, recv, ssem, rsem
-        self.half = send.shape[-1] // 2
+        self.window, self.start, self.width = window
         self.copies = {}
 
     def step(self, k):
-        n, half, far = self.n, self.half, self.n // 2
-        for d, sign in ((0, 1), (1, n - 1)):
+        far, half = self.n // 2, self.width // 2
+        everything = pl.ds(self.start, self.width)
+        for d, sign in ((0, 1), (1, -1)):
             if k < far:
                 self.copies[d, k + 1].wait_recv()
-            block = lax.rem(self.me + (sign * k) % n, n)
-            cols = pl.ds(d * half, half) if k == far else pl.ds(0, 2 * half)
+            mine = pl.ds(self.start + d * half, half)
+            other = pl.ds(self.start + (1 - d) * half, half)
 
             @pl.loop(0, self.size // 16)
-            def _(i, d=d, block=block):
+            def _(i, d=d, sign=sign):
                 rows = pl.ds(pl.multiple_of(i * 16, 16), 16)
+
+                def put(cols, add):
+                    total = self.load(sign * k, i, cols)
+                    if add:
+                        total = total + self.recv_buf[d, k, rows, cols].astype(F32)
+                    self.send_buf[d, k - 1, rows, cols] = total.astype(BF16)
+
                 if k == far:
-                    total = self.load(block, i, cols)
-                    self.send_buf[d, k - 1, rows, cols] = total.astype(BF16)
+                    put(mine, False)
                 elif k == far - 1:
-                    for h in range(2):
-                        part = pl.ds(h * half, half)
-                        total = self.load(block, i, part)
-                        if h == d:
-                            total = total + self.recv_buf[d, k, rows, part].astype(F32)
-                        self.send_buf[d, k - 1, rows, part] = total.astype(BF16)
+                    put(mine, True)
+                    put(other, False)
                 else:
-                    total = self.load(block, i, cols) + self.recv_buf[d, k, rows, :].astype(F32)
-                    self.send_buf[d, k - 1, rows, :] = total.astype(BF16)
-
+                    put(everything, True)
+
+            cols = mine if k == far else everything
             copy = remote(
                 self.send_buf.at[d, k - 1, :, cols], self.recv_buf.at[d, k - 1, :, cols],
-                self.ssem.at[d, k - 1], self.rsem.at[d, k - 1],
-                self.device(lax.rem(self.me + sign, n)),
+                self.ssem.at[self.window, d, k - 1], self.rsem.at[self.window, d, k - 1],
+                self.device(lax.rem(self.me + sign + self.n, self.n)),
             )
             copy.start()
             self.copies[d, k] = copy
 
     def finish(self, store):
+        cols = pl.ds(self.start, self.width)
         for d in range(2):
             self.copies[d, 1].wait_recv()
 
         @pl.loop(0, self.size // 16)
         def _(i):
             rows = pl.ds(pl.multiple_of(i * 16, 16), 16)
-            total = self.load(self.me, i, pl.ds(0, 2 * self.half))
+            total = self.load(0, i, cols)
             for d in range(2):
-                if self.n == 2 * 1:
-                    continue
-                total = total + self.recv_buf[d, 0, rows, :].astype(F32)
-            store(i, total)
+                total = total + self.recv_buf[d, 0, rows, cols].astype(F32)
+            store(i, cols, total)
 
     def drain(self):
         for copy in self.copies.values():
@@ -82,10 +85,10 @@
 
 
 class GatherRing:
-    def __init__(self, n, me, device, base, size, out, ssem, rsem):
+    def __init__(self, n, me, device, base, size, out, ssem, rsem, window):
         self.n, self.me, self.device, self.base, self.size = n, me, device, base, size
         self.out, self.ssem, self.rsem = out, ssem, rsem
-        self.half = out.shape[-1] // 2
+        self.window, self.start, self.width = window
         self.copies = {}
 
     def view(self, block, cols):
@@ -93,7 +96,8 @@
         return self.out.at[pl.ds(start, self.size), cols]
 
     def cols(self, d, k):
-        return pl.ds(d * self.half, self.half) if k == self.n // 2 else pl.ds(0, 2 * self.half)
+        half = self.width // 2
+        return pl.ds(self.start + d * half, half) if k == self.n // 2 else pl.ds(self.start, self.width)
 
     def source(self, d, k):
         back = (self.n - k) % self.n if d == 0 else k % self.n
@@ -103,7 +107,7 @@
         for d, sign in ((0, 1), (1, self.n - 1)):
             view = self.view(self.source(d, k - 1), self.cols(d, k))
             copy = remote(
-                view, view, self.ssem.at[d, k - 1], self.rsem.at[d, k - 1],
+                view, view, self.ssem.at[self.window, d, k - 1], self.rsem.at[self.window, d, k - 1],
                 self.device(lax.rem(self.me + sign, self.n)),
             )
             copy.start()
@@ -119,11 +123,11 @@
 
 
 def kernel(
-    emb_hbm, cen_hbm, out_hbm,
+    emb_hbm, cen_hbm, out,
     emb, cen, unit, plan, scale_b, col_acc, row_scale,
     col_v, col_c, col_x, col_z, row_v, row_r,
     mate_s, mate_r, own, own_a, own_b,
-    ax_s, ax_r, az_s, az_r, bz_s, bz_r, bx_s, bx_r, out,
+    ax_s, ax_r, az_s, az_r, bz_s, bz_r, bx_s, bx_r,
     local_sem, unit_ss, unit_rs, col_ss, col_rs, row_ss, row_rs, mate_ss, mate_rs,
     ax_ss, ax_rs, az_ss, az_rs, bz_ss, bz_rs, bx_ss, bx_rs,
     gaz_ss, gaz_rs, gax_ss, gax_rs, gbx_ss, gbx_rs, gbz_ss, gbz_rs, fwd_ss, fwd_rs,
@@ -288,14 +292,17 @@
                         part = part + p
                 col_v[t + 1, 0, pl.ds(g, 1), :] = lane_total(part)
 
-    step = 256
     mine = protos // 2
+    part = mine // 2
+    ax_size, bz_size = part // NX, part // NZ
+    size = part // (NX * NZ)
     all_unit = unit.reshape(NY * rows, width)
-
-    def partial_sums(start):
-        js = pl.ds(pl.multiple_of(start, step), step)
+    order = [(4, 3, 2), (-3, 2, 1), (-2, 1, -1), (-1, 0, 0)]
+
+    def codes(start, count):
+        js = pl.ds(pl.multiple_of(start, 64), count)
         spread = scale_b[js, :]
-        codes = jnp.concatenate(
+        return jnp.concatenate(
             [
                 (plan[b, js, h * 128 : h * 128 + 128] * spread * row_scale[2 * b + h : 2 * b + h + 1, :]).astype(BF16)
                 for b in range(NY)
@@ -303,77 +310,101 @@
             ],
             axis=1,
         )
-        return jnp.dot(codes, all_unit[...], preferred_element_type=F32)
-
-    def mate_copy(q):
-        view = pl.ds(pl.multiple_of(q * step, step), step)
-        return remote(mate_s.at[view, :], mate_r.at[view, :], mate_ss.at[q], mate_rs.at[q], mate_device)
-
-    @pl.loop(0, mine // step)
-    def _(q):
-        view = pl.ds(pl.multiple_of(q * step, step), step)
-        mate_s[view, :] = partial_sums(mate * mine + q * step).astype(BF16)
-        mate_copy(q).start()
-
-    @pl.loop(0, mine // step)
-    def _(q):
-        view = pl.ds(pl.multiple_of(q * step, step), step)
-        total = partial_sums(core * mine + q * step)
-        mate_copy(q).wait_recv()
-        own[view, :] = total + mate_r[view, :].astype(F32)
-
-    part = mine // 2
-    ax_size, bz_size = part // NX, part // NZ
-    size = part // (NX * NZ)
-
-    def loader(ref, base, size):
-        def load(block, i, cols):
-            return ref[pl.ds(pl.multiple_of(base + block * size + i * 16, 16), 16), cols]
+
+    def partial_sums(base, s):
+        first, second, third = order[s]
+        lhs = [
+            codes(base + part + lax.rem(z + first + NZ, NZ) * bz_size, bz_size),
+            codes(base + part + lax.rem(z + second + NZ, NZ) * bz_size, bz_size),
+            codes(base + lax.rem(x + third + NX, NX) * ax_size, ax_size),
+        ]
+        return jnp.dot(jnp.concatenate(lhs, axis=0), all_unit[...], preferred_element_type=F32)
+
+    mate_copies = []
+
+    def sums(s):
+        mate_s[s] = partial_sums(mate * mine, s).astype(BF16)
+        copy = remote(mate_s.at[s], mate_r.at[s], mate_ss.at[s], mate_rs.at[s], mate_device)
+        copy.start()
+        mate_copies.append(copy)
+        total = partial_sums(core * mine, s)
+        copy.wait_recv()
+        own[s] = total + mate_r[s].astype(F32)
+
+    place_b = {off: (s, i * bz_size) for s, row in enumerate(order) for i, off in enumerate(row[:2])}
+    place_a = {row[2]: (s, 2 * bz_size) for s, row in enumerate(order)}
+
+    def load_b(off, i, cols):
+        s, start = place_b[off if off in place_b else off + NZ]
+        return own[s, pl.ds(pl.multiple_of(start + i * 16, 16), 16), cols]
+
+    def load_a(off, i, cols):
+        s, start = place_a[off if off in place_a else off + NX]
+        return own[s, pl.ds(pl.multiple_of(start + i * 16, 16), 16), cols]
+
+    def loader(ref, me, n):
+        def load(off, i, cols):
+            block = lax.rem(me + off + n, n)
+            return ref[pl.ds(pl.multiple_of(block * size + i * 16, 16), 16), cols]
 
         return load
 
-    ax = ScatterRing(NX, x, x_device, loader(own, 0, ax_size), ax_size, ax_s, ax_r, ax_ss, ax_rs)
-    bz = ScatterRing(NZ, z, z_device, loader(own, part, bz_size), bz_size, bz_s, bz_r, bz_ss, bz_rs)
-    az = ScatterRing(NZ, z, z_device, loader(own_a, 0, size), size, az_s, az_r, az_ss, az_rs)
-    bx = ScatterRing(NX, x, x_device, loader(own_b, 0, size), size, bx_s, bx_r, bx_ss, bx_rs)
+    whole = (0, 0, width)
+    windows = [(w, w * (width // WINDOWS), width // WINDOWS) for w in range(WINDOWS)]
+    ax = [ScatterRing(NX, x, x_device, load_a, ax_size, ax_s, ax_r, ax_ss, ax_rs, w) for w in windows]
+    bz = [ScatterRing(NZ, z, z_device, load_b, bz_size, bz_s, bz_r, bz_ss, bz_rs, w) for w in windows]
+    az = ScatterRing(NZ, z, z_device, loader(own_a, z, NZ), size, az_s, az_r, az_ss, az_rs, whole)
+    bx = ScatterRing(NX, x, x_device, loader(own_b, x, NX), size, bx_s, bx_r, bx_ss, bx_rs, whole)
 
     def keep(ref):
-        def store(i, total):
-            ref[pl.ds(pl.multiple_of(i * 16, 16), 16), :] = total
+        def store(i, cols, total):
+            ref[pl.ds(pl.multiple_of(i * 16, 16), 16), cols] = total
 
         return store
 
     def deliver(base):
-        def store(i, total):
+        def store(i, cols, total):
             out[pl.ds(pl.multiple_of(base + i * 16, 16), 16), :] = rescale(total).astype(BF16)
 
         return store
+
+    def each(rings, k):
+        for ring in rings:
+            ring.step(k)
 
     base_a = core * mine
     base_b = base_a + part
-    bz.step(4)
-    ax.step(2)
-    bz.step(3)
-    ax.step(1)
-    bz.step(2)
-    bz.step(1)
-    ax.finish(keep(own_a))
+    sums(0)
+    each(bz, 4)
+    each(ax, 2)
+    sums(1)
+    each(bz, 3)
+    sums(2)
+    each(ax, 1)
+    sums(3)
+    each(bz, 2)
+    each(bz, 1)
+    for ring in ax:
+        ring.finish(keep(own_a))
     az.step(4)
-    bz.finish(keep(own_b))
+    for ring in bz:
+        ring.finish(keep(own_b))
     bx.step(2)
     az.step(3)
     bx.step(1)
     az.step(2)
+    bx.finish(deliver(base_b + z * bz_size + x * size))
+    gbx = GatherRing(NX, x, x_device, base_b + z * bz_size, size, out, gbx_ss, gbx_rs, whole)
+    gbx.step(1)
     az.step(1)
-    bx.finish(deliver(base_b + z * bz_size + x * size))
-    gbx = GatherRing(NX, x, x_device, base_b + z * bz_size, size, out, gbx_ss, gbx_rs)
-    gbx.step(1)
+    gbx.arrive(1)
+    gbx.step(2)
     az.finish(deliver(base_a + x * ax_size + z * size))
-    gaz = GatherRing(NZ, z, z_device, base_a + x * ax_size, size, out, gaz_ss, gaz_rs)
+    gaz = GatherRing(NZ, z, z_device, base_a + x * ax_size, size, out, gaz_ss, gaz_rs, whole)
     gaz.step(1)
 
-    gax = GatherRing(NX, x, x_device, base_a, ax_size, out, gax_ss, gax_rs)
-    gbz = GatherRing(NZ, z, z_device, base_b, bz_size, out, gbz_ss, gbz_rs)
+    gax = [GatherRing(NX, x, x_device, base_a, ax_size, out, gax_ss, gax_rs, w) for w in windows]
+    gbz = [GatherRing(NZ, z, z_device, base_b, bz_size, out, gbz_ss, gbz_rs, w) for w in windows]
     forwards = []
 
     def forward(view):
@@ -382,47 +413,37 @@
         copy.start()
         forwards.append(copy)
 
-    def forward_arrived(ring, k):
+    def arrived(ring, k):
         ring.arrive(k)
         if k < ring.n // 2:
             ring.step(k + 1)
         for d in range(2):
             forward(ring.view(ring.source(d, k), ring.cols(d, k)))
 
-    gbx.arrive(1)
-    gbx.step(2)
+    gbx.arrive(2)
+    each(gbz, 1)
+    forward(gbz[0].view(z, pl.ds(0, width)))
     gaz.arrive(1)
     gaz.step(2)
-    gbx.arrive(2)
-    gbz.step(1)
-    forward(gbz.view(z, pl.ds(0, width)))
     gaz.arrive(2)
     gaz.step(3)
+    arrived(gbz[0], 1)
     gaz.arrive(3)
     gaz.step(4)
-    forward_arrived(gbz, 1)
+    for ring in gbz[1:]:
+        arrived(ring, 1)
     gaz.arrive(4)
-    gax.step(1)
-    forward(gax.view(x, pl.ds(0, width)))
-    forward_arrived(gbz, 2)
-    forward_arrived(gax, 1)
-    forward_arrived(gbz, 3)
-    forward_arrived(gax, 2)
-    forward_arrived(gbz, 4)
+    each(gax, 1)
+    forward(gax[0].view(x, pl.ds(0, width)))
+    for rings, k in ((gbz, 2), (gax, 1), (gbz, 3), (gax, 2), (gbz, 4)):
+        for ring in rings:
+            arrived(ring, k)
     for copy in forwards:
         copy.wait_recv()
-    store = pltpu.make_async_copy(out, out_hbm, local_sem.at[2])
-    store.start()
-    for copy in ups + forwards:
+    for copy in ups + forwards + mate_copies:
         copy.wait_send()
-    for ring in (ax, bz, az, bx, gbx, gaz, gax, gbz):
+    for ring in ax + bz + [az, bx, gbx, gaz] + gax + gbz:
         ring.drain()
-
-    @pl.loop(0, mine // step)
-    def _(q):
-        mate_copy(q).wait_send()
-
-    store.wait()
 
 
 def per_device(embeddings, centres):
@@ -447,29 +468,30 @@
         VMEM((ITERS, NZ - 1, protos // 128, 128), F32),
         VMEM((ITERS, 8, 128), F32),
         VMEM((ITERS, NY - 1, 8, 128), F32),
-        VMEM((mine, width), BF16),
-        VMEM((mine, width), BF16),
-        VMEM((mine, width), F32),
+        VMEM((4, mine // 4, width), BF16),
+        VMEM((4, mine // 4, width), BF16),
+        VMEM((4, mine // 4, width), F32),
         VMEM((ax_size, width), F32),
         VMEM((bz_size, width), F32),
     ]
     for n, block in rings:
         scratch += [VMEM((2, n // 2, block, width), BF16)] * 2
-    scratch += [VMEM((protos, width), BF16)]
     pairs = [(6,), (ITERS, 1 + NX - 1 + NZ - 1), (ITERS, NY - 1), (4,)]
-    pairs += [(2, n // 2) for n, _ in rings]
-    pairs += [(2, NZ // 2), (2, NX // 2), (2, NX // 2), (2, NZ // 2), (14,)]
-    scratch += [DMA((3,))]
+    counts = [WINDOWS, 1, WINDOWS, 1]
+    pairs += [(w, 2, n // 2) for (n, _), w in zip(rings, counts)]
+    pairs += [(1, 2, NZ // 2), (WINDOWS, 2, NX // 2), (1, 2, NX // 2), (WINDOWS, 2, NZ // 2)]
+    pairs += [(2 + WINDOWS * (NX + NZ),)]
+    scratch += [DMA((2,))]
     for shape in pairs:
         scratch += [DMA(shape)] * 2
     return pl.pallas_call(
         kernel,
-        out_shape=jax.ShapeDtypeStruct((protos, width), BF16),
-        in_specs=[pl.BlockSpec(memory_space=pl.ANY)] * 2,
-        out_specs=pl.BlockSpec(memory_space=pl.ANY),
+        out_shape=VMEM((protos, width), BF16),
+        in_specs=[pl.BlockSpec(memory_space=pltpu.HBM)] * 2,
+        out_specs=pl.BlockSpec(memory_space=pltpu.VMEM),
         scratch_shapes=scratch,
         compiler_params=pltpu.CompilerParams(
-            collective_id=0, has_side_effects=True, vmem_limit_bytes=60 * 1024 * 1024
+            collective_id=0, has_side_effects=True, vmem_limit_bytes=56 * 1024 * 1024
         ),
     )(embeddings, centres)
 

time: 153 us -> 147 us (0.961)
  Pallas kernels: 149 us -> 145 us
  local copies, waits for them, and re-layouts: 4.64 us -> 2.02 us
    pallas_call x1, Pallas kernels: 149 us -> 145 us  [per_device(): pl.pallas_call(kernel, out_shape=VMEM((protos, width), BF16), in_specs=[p...]
    unnamed x1, local copies, waits for them, and re-layouts: 4.64 us -> 2.02 us
where the time goes in v2:
time: 147 us
  Pallas kernels  145 us (99%)
  local copies, waits for them, and re-layouts  2.02 us (1%)
    pallas_call x1, Pallas kernels, per_device(): pl.pallas_call(kernel, out_shape=VMEM((protos, width), BF16), in_specs=[p...  145 us

profile of v2, /device:TPU:1, one launch (start us, length us, event | category | flops | bytes accessed | tf_op | source)
XLA Modules:
  0.0 146.9 jit_solution(13613962160968269676)
XLA Ops:
  0.0 144.9 %shard_map.28 = bf16[2048,1024]{1,0:T(8,128)(2,1)S(1)} custom-call(bf16[256,1024]{1,0:T(8,128)(2,1)} %emb_hbm.1, bf16[2048,1024]{1,0:T(8,128)(2,1)} %cen_hbm.1), custom_call_target="tpu_custom_call" | custom-call | tf_op jit(solution)/shard_map/pallas_call | solution.py:487
  144.9 2.0 %copy.4 = bf16[2048,1024]{1,0:T(8,128)(2,1)} copy(bf16[2048,1024]{1,0:T(8,128)(2,1)S(1)} %shard_map.28) | data formatting | bytes 8388608

commit v3 on v2

--- a/solution.py
+++ b/solution.py
@@ -150,9 +150,9 @@
         return at(x, k, core)
 
     mate_device = at(x, z, mate)
-    x_peers = [x_device(lax.rem(x + k, NX)) for k in range(1, NX)]
-    z_peers = [z_device(lax.rem(z + k, NZ)) for k in range(1, NZ)]
-    y_peers = [(dp, lax.rem(y + k, NY)) for k in range(1, NY)]
+    x_peers = [x_device(lax.rem(x + k, NX)) for k in (2, 1, 3)]
+    z_peers = [z_device(lax.rem(z + k, NZ)) for k in (4, 3, 5, 2, 6, 1, 7)]
+    y_peers = [(dp, lax.rem(y + k, NY)) for k in (2, 1, 3)]
     peers = [mate_device] + x_peers + z_peers + y_peers
 
     load_emb = pltpu.make_async_copy(emb_hbm, emb, local_sem.at[0])
@@ -181,7 +181,7 @@
         return copy
 
     def scores(block, first):
-        step = 256
+        step = 1024
 
         @pl.loop(0, protos // step)
         def _(i):
@@ -320,27 +320,31 @@
         ]
         return jnp.dot(jnp.concatenate(lhs, axis=0), all_unit[...], preferred_element_type=F32)
 
-    mate_copies = []
+    def mate_copy(s):
+        return remote(mate_s.at[s], mate_r.at[s], mate_ss.at[s], mate_rs.at[s], mate_device)
 
     def sums(s):
-        mate_s[s] = partial_sums(mate * mine, s).astype(BF16)
-        copy = remote(mate_s.at[s], mate_r.at[s], mate_ss.at[s], mate_rs.at[s], mate_device)
-        copy.start()
-        mate_copies.append(copy)
-        total = partial_sums(core * mine, s)
-        copy.wait_recv()
-        own[s] = total + mate_r[s].astype(F32)
+        @pl.when(core < NC)
+        def _():
+            mate_s[s] = partial_sums(mate * mine, s).astype(BF16)
+            mate_copy(s).start()
+
+        @pl.when(core < NC)
+        def _():
+            own[s] = partial_sums(core * mine, s)
 
     place_b = {off: (s, i * bz_size) for s, row in enumerate(order) for i, off in enumerate(row[:2])}
     place_a = {row[2]: (s, 2 * bz_size) for s, row in enumerate(order)}
 
     def load_b(off, i, cols):
         s, start = place_b[off if off in place_b else off + NZ]
-        return own[s, pl.ds(pl.multiple_of(start + i * 16, 16), 16), cols]
+        rows = pl.ds(pl.multiple_of(start + i * 16, 16), 16)
+        return own[s, rows, cols] + mate_r[s, rows, cols].astype(F32)
 
     def load_a(off, i, cols):
         s, start = place_a[off if off in place_a else off + NX]
-        return own[s, pl.ds(pl.multiple_of(start + i * 16, 16), 16), cols]
+        rows = pl.ds(pl.multiple_of(start + i * 16, 16), 16)
+        return own[s, rows, cols] + mate_r[s, rows, cols].astype(F32)
 
     def loader(ref, me, n):
         def load(off, i, cols):
@@ -375,13 +379,17 @@
     base_a = core * mine
     base_b = base_a + part
     sums(0)
+    sums(1)
+    mate_copy(0).wait_recv()
     each(bz, 4)
     each(ax, 2)
-    sums(1)
+    sums(2)
+    mate_copy(1).wait_recv()
+    sums(3)
     each(bz, 3)
-    sums(2)
+    mate_copy(2).wait_recv()
     each(ax, 1)
-    sums(3)
+    mate_copy(3).wait_recv()
     each(bz, 2)
     each(bz, 1)
     for ring in ax:
@@ -440,7 +448,7 @@
             arrived(ring, k)
     for copy in forwards:
         copy.wait_recv()
-    for copy in ups + forwards + mate_copies:
+    for copy in ups + forwards + [mate_copy(s) for s in range(4)]:
         copy.wait_send()
     for ring in ax + bz + [az, bx, gbx, gaz] + gax + gbz:
         ring.drain()

time: 147 us -> 140 us (0.952)
  Pallas kernels: 145 us -> 138 us
    pallas_call x1, Pallas kernels: 145 us -> 138 us  [per_device(): pl.pallas_call(kernel, out_shape=VMEM((protos, width), BF16), in_specs=[p...]
where the time goes in v3:
time: 140 us
  Pallas kernels  138 us (99%)
  local copies, waits for them, and re-layouts  2.02 us (1%)
    pallas_call x1, Pallas kernels, per_device(): pl.pallas_call(kernel, out_shape=VMEM((protos, width), BF16), in_specs=[p...  138 us

profile of v3, /device:TPU:1, one launch (start us, length us, event | category | flops | bytes accessed | tf_op | source)
XLA Modules:
  0.0 140.0 jit_solution(14179105921656705798)
XLA Ops:
  0.0 137.9 %shard_map.28 = bf16[2048,1024]{1,0:T(8,128)(2,1)S(1)} custom-call(bf16[256,1024]{1,0:T(8,128)(2,1)} %emb_hbm.1, bf16[2048,1024]{1,0:T(8,128)(2,1)} %cen_hbm.1), custom_call_target="tpu_custom_call" | custom-call | tf_op jit(solution)/shard_map/pallas_call | solution.py:495
  137.9 2.0 %copy.4 = bf16[2048,1024]{1,0:T(8,128)(2,1)} copy(bf16[2048,1024]{1,0:T(8,128)(2,1)S(1)} %shard_map.28) | data formatting | bytes 8388608
